TPU v7x, 256 devices: a whole 4x4x8 slice. The times are simulated.
256 devices in a mesh: section: 4 (over x), dp: 64 (over y, z, core).
Axes of the slice: x: 4, y: 4, z: 8, core: 2. Of those that a mesh axis runs over, the one named last changes fastest.
Arguments:
- section_inputs: bfloat16 [4, 8192, 4096], P('section', 'dp'), may hold values from -6 to 6
- gains: float32 [4, 4096], P('section'), may hold values from 0.25 to 1.75
- value_weight: bfloat16 [4, 4096, 1024], P('section', 'dp'), may hold values from -0.09375 to 0.09375
- top_cotangent: bfloat16 [8192, 4096], P('dp'), may hold values from -16 to 16
- proxy_loss: float32 [8192], P('dp'), may hold values from 0.5 to 5.5
- reference_loss: float32 [8192], P('dp'), may hold values from 1 to 3
- lengths: int32 [64, 8], P('dp'), may hold values from 1 to 80, 128 in all within a row
- doc_domain: int32 [64, 8], P('dp'), may hold values from 0 to 21
- log_weights: float32 [22], replicated, may hold values from -4 to -1
- step_count: int32 [1], replicated, may hold values from 1 to 256
Outputs:
- section_grads: bfloat16 [4, 8192, 4096], P('section', 'dp')
- weight_grads: float32 [4, 4096, 1024], P('section', 'dp')
- new_log_weights: float32 [22], replicated
Inputs may be any that keep to these rules, and one draw needn't show every extreme that they name: `lengths`: each row sums to 128: the documents fill their pack in order.
All inputs are finite; a program needn't handle non-finite values.
Results may differ from a plain program's by a relative error of at most 0.0071.
Values may be sent and summed in bfloat16 or wider, within the bound.
No kernel may reach another device: no remote copies, remote signals or barrier semaphores. Data moves between devices by JAX's collectives and lax.ppermute only.
A program may use at most 128 MiB of HBM per device.

v0:
```python
import jax
import jax.numpy as jnp
from jax import lax
from jax.experimental import pallas as pl
from jax.experimental.pallas import tpu as pltpu
from jax.sharding import Mesh
from jax.sharding import PartitionSpec as P

DOMAINS = 22
MICRO = 4
SECTIONS = 4
DOCS = 8


EPS = 1e-05
SMOOTH = 0.001
Y, Z, CORE = 4, 8, 2
STEP = 1024
STEP_IN = 2048
STEP_OUT = 2048
STEP_END = 512
LAG = 3
VMEM_LIMIT = 24 * 1024 * 1024


DP = ("y", "z", "core")


def shifted(value, axis, by):
    size = lax.axis_size(axis)
    return lax.ppermute(value, axis, [(i, (i + by) % size) for i in range(size)])


def summed(value):
    for axis in ("core", "z", "y"):
        size = lax.axis_size(axis)
        copies = jnp.broadcast_to(value[None], (size,) + value.shape)
        value = jnp.sum(lax.all_to_all(copies, axis, 0, 0, tiled=True), axis=0)
    return value


def ring_scatter(block, size, axis):
    def pair(high, low):
        high, low = lax.optimization_barrier(
            (high.astype(jnp.bfloat16), low.astype(jnp.bfloat16))
        )
        high, low = shifted(high, axis, 1), shifted(low, axis, -1)
        return high.astype(jnp.float32), low.astype(jnp.float32)

    far = block(size // 2)
    half = far.shape[0] // 2
    up, down = pair(far[:half], far[half:])
    zero = jnp.zeros_like(up)
    up = jnp.concatenate([up, zero], axis=0)
    down = jnp.concatenate([zero, down], axis=0)
    for offset in range(size // 2 - 1, 0, -1):
        up, down = pair(block(offset) + up, block(-offset) + down)
    return block(0) + up + down


def swapped(blocks, axis):
    got = lax.all_to_all(blocks.astype(jnp.bfloat16), axis, 0, 0, tiled=True)
    total = got[0].astype(jnp.float32)
    for i in range(1, got.shape[0]):
        total = total + got[i].astype(jnp.float32)
    return total


def scattered(left, right):
    depth, cols = left.shape[1], right.shape[1]
    half = cols // 2
    unit = depth // (Y * Z)
    first = jnp.einsum("td,tk->dk", left, right[:, :half], preferred_element_type=jnp.float32)
    first = first.astype(jnp.bfloat16)
    later, first = lax.optimization_barrier((right[:, half:], first))
    first = swapped(first.reshape(Y, Z * unit, half), "y")
    second = jnp.einsum("td,tk->dk", left, later, preferred_element_type=jnp.float32)
    second = second.reshape(Y, Z, unit, half)
    here = lax.axis_index("z")

    def block(offset):
        piece = lax.dynamic_slice_in_dim(second, (here + offset) % Z, 1, 1)
        return piece.reshape(Y * unit, half)

    second = ring_scatter(block, Z, "z")
    first = swapped(first.reshape(Z, unit, half), "z")
    second = swapped(second.reshape(Y, unit, half), "y")
    return jnp.concatenate([first, second], axis=1)


def local_statistics(proxy_loss, reference_loss, lengths, doc_domain):
    rows = proxy_loss.shape[0]
    ends = jnp.cumsum(lengths[0])
    position = jnp.arange(rows, dtype=jnp.int32)
    doc_index = jnp.sum((position[:, None] >= ends[None, :]).astype(jnp.int32), axis=1)
    doc_hot = doc_index[:, None] == jnp.arange(DOCS, dtype=jnp.int32)[None, :]
    end_of = jnp.sum(jnp.where(doc_hot, ends[None, :], 0), axis=1)
    live = position + 1 != end_of
    domain = jnp.sum(jnp.where(doc_hot, doc_domain[0][None, :], 0), axis=1)
    onehot = (domain[:, None] == jnp.arange(DOMAINS, dtype=jnp.int32)[None, :]).astype(jnp.float32)
    selected = (live & (proxy_loss > reference_loss)).astype(jnp.float32)
    excess = selected * (proxy_loss - reference_loss)
    excess_part = jnp.sum(onehot * excess[:, None], axis=0)
    count_part = jnp.sum(onehot * live.astype(jnp.float32)[:, None], axis=0)
    return (onehot, selected, excess_part, count_part)


def domain_weights(statistics, log_weights, step_count, total_tokens):
    onehot, selected, excess_part, count_part = statistics
    parts = jnp.zeros((8, 128), jnp.float32)
    parts = parts.at[0, :DOMAINS].set(excess_part).at[1, :DOMAINS].set(count_part)
    parts = summed(parts)
    excess_sum, count = parts[0, :DOMAINS], parts[1, :DOMAINS]
    counts = jnp.maximum(count, 1.0)
    mean_excess = excess_sum / counts
    rate = 1.0 / jnp.sqrt(step_count[0].astype(jnp.float32))
    logits = log_weights + rate * mean_excess
    new_log = logits - jnp.log(jnp.sum(jnp.exp(logits)))
    lam = (1.0 - SMOOTH) * jnp.exp(new_log) + SMOOTH / DOMAINS
    per_domain = lam * total_tokens / counts
    weight = jnp.sum(onehot * per_domain[None, :], axis=1) * selected
    return (weight, new_log)


def forward_kernel(x_ref, r_ref, gamma_ref, w_ref, normed_ref, slope_ref, hidden_ref):
    depth = x_ref.shape[1]
    step = min(STEP, depth)
    slope_ref[...] = jnp.zeros_like(slope_ref)

    @pl.loop(0, depth // step)
    def _(i):
        cols = pl.ds(pl.multiple_of(i * step, step), step)
        x = x_ref[:, cols].astype(jnp.float32)
        normed = (x * r_ref[...] * gamma_ref[:, cols]).astype(jnp.bfloat16)
        normed_ref[:, cols] = normed
        slope_ref[...] += jnp.dot(normed, w_ref[cols, :], preferred_element_type=jnp.float32)

    act = slope_ref[...]
    sig = jax.nn.sigmoid(act)
    hidden_ref[...] = (act * sig).astype(jnp.bfloat16)
    slope_ref[...] = sig * (1.0 + act * (1.0 - sig))


def forward(x, inverse, gamma, weight):
    rows, depth = x.shape
    width = weight.shape[1]
    spec = pl.BlockSpec(memory_space=pltpu.VMEM)
    return pl.pallas_call(
        forward_kernel,
        in_specs=[spec] * 4,
        out_specs=[spec] * 3,
        out_shape=[
            jax.ShapeDtypeStruct((rows, depth), jnp.bfloat16),
            jax.ShapeDtypeStruct((rows, width), jnp.float32),
            jax.ShapeDtypeStruct((rows, width), jnp.bfloat16),
        ],
        compiler_params=pltpu.CompilerParams(vmem_limit_bytes=VMEM_LIMIT),
        cost_estimate=pl.CostEstimate(
            flops=2 * rows * depth * width, bytes_accessed=2 * depth * width, transcendentals=0
        ),
        name="forward",
    )(x, inverse, gamma, weight)


def tick_kernel(
    index_ref,
    section_ref,
    came_ref,
    top_ref,
    x_ref,
    r_ref,
    weight_ref,
    slope_ref,
    gamma_ref,
    w_ref,
    old_dx_ref,
    old_wg_ref,
    old_wa_ref,
    out_ref,
    dx_ref,
    wg_ref,
    wa_ref,
    cot_ref,
    scaled_ref,
    dx_block,
    wg_block,
    wa_block,
    sems,
):
    block, depth = came_ref.shape
    index = index_ref[0]
    is_top = section_ref[0] == SECTIONS - 1

    @pl.when((index >= 0) & (index < MICRO))
    def _():
        rows = pl.ds(pl.multiple_of(index * block, block), block)

        @pl.when(is_top)
        def _():
            cot_ref[...] = top_ref[rows, :]

        @pl.when(jnp.logical_not(is_top))
        def _():
            cot_ref[...] = came_ref[...]

        weight = weight_ref[rows, :]
        wg_block[...] = (weight * cot_ref[...].astype(jnp.float32)).astype(jnp.bfloat16)
        wg_copy = pltpu.make_async_copy(wg_block, wg_ref.at[rows, :], sems.at[0])
        wg_copy.start()
        step = min(STEP_IN, depth)

        def into(i, total):
            cols = pl.ds(pl.multiple_of(i * step, step), step)
            return total + jnp.dot(
                cot_ref[:, cols], w_ref[cols, :], preferred_element_type=jnp.float32
            )

        grad_h = lax.fori_loop(
            0, depth // step, into, jnp.zeros((block, w_ref.shape[1]), jnp.float32)
        )
        grad_a = grad_h * slope_ref[rows, :]
        wa_block[...] = (weight * grad_a).astype(jnp.bfloat16)
        wa_copy = pltpu.make_async_copy(wa_block, wa_ref.at[rows, :], sems.at[1])
        wa_copy.start()
        rounded = grad_a.astype(jnp.bfloat16)
        stride = min(STEP_OUT, depth)

        def back(i, dots):
            cols = pl.ds(pl.multiple_of(i * stride, stride), stride)
            grad_n = lax.dot_general(
                rounded,
                w_ref[cols, :],
                (((1,), (1,)), ((), ())),
                preferred_element_type=jnp.float32,
            )
            scaled = gamma_ref[:, cols] * grad_n
            scaled_ref[:, cols] = scaled
            prod = x_ref[rows, cols].astype(jnp.float32) * scaled
            return dots + jnp.sum(prod, axis=1, keepdims=True)

        dots = lax.fori_loop(0, depth // stride, back, jnp.zeros((block, 1), jnp.float32))
        r = r_ref[rows, :]
        pull = r * r * r * (dots / depth)
        span = min(STEP_END, depth)

        @pl.loop(0, depth // span)
        def _(i):
            cols = pl.ds(pl.multiple_of(i * span, span), span)
            cot = cot_ref[:, cols].astype(jnp.float32)
            x = x_ref[rows, cols].astype(jnp.float32)
            passed = (cot + r * scaled_ref[:, cols] - x * pull).astype(jnp.bfloat16)
            out_ref[:, cols] = passed
            dx_block[:, cols] = (weight * passed.astype(jnp.float32)).astype(jnp.bfloat16)

        dx_copy = pltpu.make_async_copy(dx_block, dx_ref.at[rows, :], sems.at[2])
        dx_copy.start()
        wg_copy.wait()
        wa_copy.wait()
        dx_copy.wait()


def tick(index, section, came, top, x, inverse, weight, slope, gamma, w, dx, wg, wa):
    block, depth = came.shape
    width = slope.shape[1]
    spec = pl.BlockSpec(memory_space=pltpu.VMEM)
    scalar = pl.BlockSpec(memory_space=pltpu.SMEM)
    return pl.pallas_call(
        tick_kernel,
        in_specs=[scalar] * 2 + [spec] * 8 + [pl.BlockSpec(memory_space=pl.ANY)] * 3,
        out_specs=[spec] + [pl.BlockSpec(memory_space=pl.ANY)] * 3,
        scratch_shapes=[
            pltpu.VMEM((block, depth), jnp.bfloat16),
            pltpu.VMEM((block, depth), jnp.float32),
            pltpu.VMEM((block, depth), jnp.bfloat16),
            pltpu.VMEM((block, depth), jnp.bfloat16),
            pltpu.VMEM((block, width), jnp.bfloat16),
            pltpu.SemaphoreType.DMA((3,)),
        ],
        out_shape=[
            jax.ShapeDtypeStruct((block, depth), jnp.bfloat16),
            jax.ShapeDtypeStruct(dx.shape, dx.dtype),
            jax.ShapeDtypeStruct(wg.shape, wg.dtype),
            jax.ShapeDtypeStruct(wa.shape, wa.dtype),
        ],
        input_output_aliases={10: 1, 11: 2, 12: 3},
        compiler_params=pltpu.CompilerParams(vmem_limit_bytes=VMEM_LIMIT),
        cost_estimate=pl.CostEstimate(
            flops=4 * 128 * depth * width, bytes_accessed=2 * depth * width, transcendentals=0
        ),
        name="tick",
    )(index, section, came, top, x, inverse, weight, slope, gamma, w, dx, wg, wa)


def local(
    section_inputs,
    gains,
    value_weight,
    top_cotangent,
    proxy_loss,
    reference_loss,
    lengths,
    doc_domain,
    log_weights,
    step_count,
):
    sections = lax.axis_size("section")
    section = lax.axis_index("section").astype(jnp.int32)[None]
    devices = Y * Z * CORE
    core = lax.axis_index("core")
    x = section_inputs[0]
    shard = value_weight[0]
    rows, depth = x.shape
    width = shard.shape[1]
    block = rows // MICRO
    total_tokens = rows * devices
    statistics = local_statistics(proxy_loss, reference_loss, lengths, doc_domain)
    weight, new_log = domain_weights(statistics, log_weights, step_count, total_tokens)
    weight = weight[:, None]
    xfull = x.astype(jnp.float32)
    inverse = lax.rsqrt(jnp.mean(xfull * xfull, axis=1, keepdims=True) + EPS)
    inverse, weight = lax.optimization_barrier((inverse, weight))
    full_weight = lax.all_gather(shard, DP, axis=0, tiled=True)
    normed, slope, hidden = forward(x, inverse, gains, full_weight)
    dx = jnp.zeros((rows, depth), jnp.bfloat16)
    wg = jnp.zeros((rows, depth), jnp.bfloat16)
    wa = jnp.zeros((rows, width), jnp.bfloat16)
    sent = {}
    ticks = MICRO + LAG * (sections - 1)
    for slot in range(ticks):
        came = sent[slot - LAG] if slot >= LAG else jnp.zeros((block, depth), jnp.bfloat16)
        out, dx, wg, wa = tick(
            section + (slot - LAG * (sections - 1)) + (LAG - 1) * section,
            section,
            came,
            top_cotangent,
            x,
            inverse,
            weight,
            slope,
            gains,
            full_weight,
            dx,
            wg,
            wa,
        )
        pairs = [
            (s, s - 1)
            for s in range(1, sections)
            if 0 <= slot - LAG * (sections - 1 - s) < MICRO
        ]
        if pairs:
            sent[slot] = lax.ppermute(out, "section", pairs)
    left = jnp.concatenate([normed, wg], axis=0)
    right = jnp.concatenate([wa, hidden], axis=0)
    left = jnp.concatenate([left, shifted(left, "core", 1)], axis=0)
    halves = right.reshape(2 * rows, CORE, width // CORE).transpose(1, 0, 2)
    halves = lax.all_to_all(halves, "core", 0, 0, tiled=True)
    order = jnp.where(core == 0, halves, halves[::-1])
    right = order.reshape(CORE * 2 * rows, width // CORE)
    part = scattered(left, right) * (1.0 / devices)
    pieces = lax.all_to_all(part.reshape(CORE, -1, width // CORE), "core", 0, 0, tiled=True)
    grad_shard = pieces.transpose(1, 0, 2).reshape(shard.shape)
    return (dx[None], grad_shard[None], new_log)


def solution(mesh):
    grid = Mesh(mesh.devices.reshape(-1, Y, Z, CORE), ("section",) + DP)
    return jax.shard_map(
        local,
        mesh=grid,
        in_specs=(
            P("section", DP, None),
            P("section", None),
            P("section", DP, None),
            P(DP, None),
            P(DP),
            P(DP),
            P(DP, None),
            P(DP, None),
            P(),
            P(),
        ),
        out_specs=(P("section", DP, None), P("section", DP, None), P()),
        check_vma=False,
    )
```

profile of v0, /device:TPU:1, one launch (start us, length us, event | category | flops | bytes accessed | tf_op | source)
XLA Modules:
  0.0 275.7 jit_solution(14976678810685434815)
XLA Ops:
  10.6 6.6 %all_to_all.40 = f32[2,8,128]{2,1,0:T(8,128)S(1)} all-to-all(f32[2,8,128]{2,1,0:T(8,128)S(1)} %broadcast_in_dim.68), channel_id=1, replica_groups=mesh['section'=4,'y'=4,'z'=8,'core'=2] {'core'}, dimensions={0} | all-to-all | bytes 16384 | tf_op jit(solution)/shard_map/all_to_all | solution.py:38
  17.1 13.2 %all_to_all.41 = f32[8,8,128]{2,1,0:T(8,128)S(1)} all-to-all(f32[8,8,128]{2,1,0:T(8,128)S(1)} %broadcast_in_dim.69), channel_id=1, replica_groups=mesh['section'=4,'y'=4,'z'=8,'core'=2] {'z'}, dimensions={0} | all-to-all | bytes 65536 | tf_op jit(solution)/shard_map/all_to_all | solution.py:38
  31.0 4.2 %all-to-all-start.2 = ((f32[4,8,128]{2,1,0:T(8,128)}), f32[4,8,128]{2,1,0:T(8,128)S(1)}, u32[]{:S(2)}, u32[]{:S(2)}) async-start(f32[4,8,128]{2,1,0:T(8,128)} %broadcast_in_dim.70), calls=%async_computation.2 | async-start | bytes 32768 | tf_op jit(solution)/shard_map/all_to_all | solution.py:38
  42.8 55.2 %all-gather.3.cloned.1.call-done = bf16[1,4096,1024]{2,1,0:T(8,128)(2,1)} async-done(((bf16[1,64,1024]{2,1,0:T(8,128)(2,1)}), bf16[1,4096,1024]{2,1,0:T(8,128)(2,1)}) %all-gather.3.cloned.1.call-update) | async-done | bytes 8388624 | tf_op jit(solution)/shard_map/all_gather | solution.py:322
  98.0 3.4 %copy-done = bf16[1,4096,1024]{2,1,0:T(8,128)(2,1)S(1)} copy-done((bf16[1,4096,1024]{2,1,0:T(8,128)(2,1)S(1)}, bf16[1,4096,1024]{2,1,0:T(8,128)(2,1)}, u32[]{:S(2)}) %copy-start) | copy-done | bytes 8388632
  103.3 2.2 forward.1
  115.5 35.8 %collective-permute-done.4.came_ref = bf16[32,4096]{1,0:T(8,128)(2,1)S(1)} collective-permute-done((bf16[32,4096]{1,0:T(8,128)(2,1)S(1)}, bf16[32,4096]{1,0:T(8,128)(2,1)S(1)}, u32[]{:S(2)}, u32[]{:S(2)}) %collective-permute-start.4) | collective-permute-done | bytes 262176 | tf_op jit(solution)/shard_map/ppermute | solution.py:352
  151.3 6.2 %tick.22 = (bf16[32,4096]{1,0:T(8,128)(2,1)S(1)}, bf16[128,4096]{1,0:T(8,128)(2,1)}, bf16[128,4096]{1,0:T(8,128)(2,1)S(1)}, bf16[128,1024]{1,0:T(8,128)(2,1)S(1)}) custom-call(s32[1]{0:T(128)S(6)} %add.279.index_ref, s32[1]{0:T(128)} %bitcast.section_ref, ...), custom_call_target="tpu_custom_call", output_to_operand_aliasing={{1}: (10, {}), {2}: (11, {}), {3}: (12, {})} | custom-call | flops 2147483648 | bytes 8388608 | tf_op jit(solution)/shard_map/tick/pallas_call | solution.py:267
  158.8 6.9 %tick.23 = (bf16[32,4096]{1,0:T(8,128)(2,1)}, bf16[128,4096]{1,0:T(8,128)(2,1)}, bf16[128,4096]{1,0:T(8,128)(2,1)S(1)}, bf16[128,1024]{1,0:T(8,128)(2,1)S(1)}) custom-call(s32[1]{0:T(128)S(6)} %add.307.index_ref, s32[1]{0:T(128)} %bitcast.section_ref, ...), custom_call_target="tpu_custom_call", output_to_operand_aliasing={{1}: (10, {}), {2}: (11, {}), {3}: (12, {})} | custom-call | flops 2147483648 | bytes 8388608 | tf_op jit(solution)/shard_map/tick/pallas_call | solution.py:267
  166.3 6.9 %tick.24 = (bf16[32,4096]{1,0:T(8,128)(2,1)}, bf16[128,4096]{1,0:T(8,128)(2,1)}, bf16[128,4096]{1,0:T(8,128)(2,1)S(1)}, bf16[128,1024]{1,0:T(8,128)(2,1)S(1)}) custom-call(s32[1]{0:T(128)S(6)} %add.305.index_ref, s32[1]{0:T(128)} %bitcast.section_ref, ...), custom_call_target="tpu_custom_call", output_to_operand_aliasing={{1}: (10, {}), {2}: (11, {}), {3}: (12, {})} | custom-call | flops 2147483648 | bytes 8388608 | tf_op jit(solution)/shard_map/tick/pallas_call | solution.py:267
  173.9 6.9 %tick.25 = (bf16[32,4096]{1,0:T(8,128)(2,1)}, bf16[128,4096]{1,0:T(8,128)(2,1)}, bf16[128,4096]{1,0:T(8,128)(2,1)S(1)}, bf16[128,1024]{1,0:T(8,128)(2,1)S(1)}) custom-call(s32[1]{0:T(128)S(6)} %add.278.index_ref, s32[1]{0:T(128)} %bitcast.section_ref, ...), custom_call_target="tpu_custom_call", output_to_operand_aliasing={{1}: (10, {}), {2}: (11, {}), {3}: (12, {})} | custom-call | flops 2147483648 | bytes 8388608 | tf_op jit(solution)/shard_map/tick/pallas_call | solution.py:267
  184.4 4.2 %all_to_all.42 = bf16[2,256,512]{2,1,0:T(8,128)(2,1)S(1)} all-to-all(bf16[2,256,512]{2,1,0:T(8,128)(2,1)S(1)} %bitcast.109), channel_id=1, replica_groups=mesh['section'=4,'y'=4,'z'=8,'core'=2] {'core'}, dimensions={0} | all-to-all | bytes 1048576 | tf_op jit(solution)/shard_map/all_to_all | solution.py:357
  190.6 2.7 convolution_convert_fusion
  199.4 2.4 collective-permute-done.11
  204.1 3.6 %all-to-all-start.4 = ((bf16[4,1024,256]{2,1,0:T(8,128)(2,1)}), bf16[4,1024,256]{2,1,0:T(8,128)(2,1)S(1)}, u32[]{:S(2)}, u32[]{:S(2)}) async-start(bf16[4,1024,256]{2,1,0:T(8,128)(2,1)} %bitcast.107), calls=%async_computation.4 | async-start | bytes 4194304 | tf_op jit(solution)/shard_map/all_to_all | solution.py:62
  213.5 4.1 %collective-permute-done.16 = bf16[512,256]{1,0:T(8,128)(2,1)S(1)} collective-permute-done((bf16[512,256]{1,0:T(8,128)(2,1)S(1)}, bf16[512,256]{1,0:T(8,128)(2,1)S(1)}, u32[]{:S(2)}, u32[]{:S(2)}) %collective-permute-start.16) | collective-permute-done | bytes 262176 | tf_op jit(solution)/shard_map/ppermute | solution.py:31
  220.2 2.7 collective-permute-start.18
  222.9 4.1 %collective-permute-done.17 = bf16[512,256]{1,0:T(8,128)(2,1)S(1)} collective-permute-done((bf16[512,256]{1,0:T(8,128)(2,1)S(1)}, bf16[512,256]{1,0:T(8,128)(2,1)S(1)}, u32[]{:S(2)}, u32[]{:S(2)}) %collective-permute-start.17) | collective-permute-done | bytes 262176 | tf_op jit(solution)/shard_map/ppermute | solution.py:31
  227.7 4.3 %all-to-all-done.4 = bf16[4,1024,256]{2,1,0:T(8,128)(2,1)S(1)} async-done(((bf16[4,1024,256]{2,1,0:T(8,128)(2,1)}), bf16[4,1024,256]{2,1,0:T(8,128)(2,1)S(1)}, u32[]{:S(2)}, u32[]{:S(2)}) %all-to-all-start.4) | async-done | bytes 2097184 | tf_op jit(solution)/shard_map/all_to_all | solution.py:62
  232.0 3.4 %all-to-all-start.6 = ((bf16[4,128,256]{2,1,0:T(8,128)(2,1)}), bf16[4,128,256]{2,1,0:T(8,128)(2,1)S(1)}, u32[]{:S(2)}, u32[]{:S(2)}) async-start(bf16[4,128,256]{2,1,0:T(8,128)(2,1)} %bitcast.29), calls=%async_computation.6 | async-start | bytes 524288 | tf_op jit(solution)/shard_map/all_to_all | solution.py:62
  236.5 4.4 %all-to-all-done.6 = bf16[4,128,256]{2,1,0:T(8,128)(2,1)S(1)} async-done(((bf16[4,128,256]{2,1,0:T(8,128)(2,1)}), bf16[4,128,256]{2,1,0:T(8,128)(2,1)S(1)}, u32[]{:S(2)}, u32[]{:S(2)}) %all-to-all-start.6) | async-done | bytes 262176 | tf_op jit(solution)/shard_map/all_to_all | solution.py:62
  240.9 4.6 %all-to-all-start.5 = ((bf16[8,128,256]{2,1,0:T(8,128)(2,1)}), bf16[8,128,256]{2,1,0:T(8,128)(2,1)S(1)}, u32[]{:S(2)}, u32[]{:S(2)}) async-start(bf16[8,128,256]{2,1,0:T(8,128)(2,1)} %bitcast.17), calls=%async_computation.5 | async-start | bytes 1048576 | tf_op jit(solution)/shard_map/all_to_all | solution.py:62
  245.6 11.8 %all-to-all-done.5 = bf16[8,128,256]{2,1,0:T(8,128)(2,1)S(1)} async-done(((bf16[8,128,256]{2,1,0:T(8,128)(2,1)}), bf16[8,128,256]{2,1,0:T(8,128)(2,1)S(1)}, u32[]{:S(2)}, u32[]{:S(2)}) %all-to-all-start.5) | async-done | bytes 524320 | tf_op jit(solution)/shard_map/all_to_all | solution.py:62
  257.4 10.2 %all_to_all.43 = f32[2,64,512]{2,1,0:T(8,128)S(1)} all-to-all(f32[2,64,512]{2,1,0:T(8,128)S(1)} %maximum_multiply_fusion), channel_id=1, replica_groups=mesh['section'=4,'y'=4,'z'=8,'core'=2] {'core'}, dimensions={0} | all-to-all | bytes 524288 | tf_op jit(solution)/shard_map/all_to_all | solution.py:361
  (102 shorter events, 50.0 us)
Async XLA Ops:
  7.2 90.8 %all-gather.3.cloned.1.call-start = ((), (), s32[]{:S(2)}) async-start(), calls=%async_computation.8 | async-start | bytes 8519680 | tf_op jit(solution)/shard_map/all_gather | solution.py:322
  31.0 8.4 %all-to-all-start.2 = ((f32[4,8,128]{2,1,0:T(8,128)}), f32[4,8,128]{2,1,0:T(8,128)S(1)}, u32[]{:S(2)}, u32[]{:S(2)}) async-start(f32[4,8,128]{2,1,0:T(8,128)} %broadcast_in_dim.70), calls=%async_computation.2 | async-start | bytes 32768 | tf_op jit(solution)/shard_map/all_to_all | solution.py:38
  106.8 2.2 collective-permute-start
  107.6 2.2 collective-permute-start.3
  108.3 2.2 collective-permute-start.2
  109.1 2.2 collective-permute-start.1
  109.8 3.0 %collective-permute-start.6 = (bf16[32,4096]{1,0:T(8,128)(2,1)S(1)}, bf16[32,4096]{1,0:T(8,128)(2,1)S(1)}, u32[]{:S(2)}, u32[]{:S(2)}) collective-permute-start(bf16[32,4096]{1,0:T(8,128)(2,1)S(1)} %get-tuple-element.118), channel_id=1, source_target_pairs={{128,64},{129,65},{130,66},{131,67},{132,68},{133,69},{134,70},{13... | collective-permute-start | bytes 786440 | tf_op jit(solution)/shard_map/ppermute | solution.py:352
  110.5 3.6 %collective-permute-start.5 = (bf16[32,4096]{1,0:T(8,128)(2,1)S(1)}, bf16[32,4096]{1,0:T(8,128)(2,1)S(1)}, u32[]{:S(2)}, u32[]{:S(2)}) collective-permute-start(bf16[32,4096]{1,0:T(8,128)(2,1)S(1)} %get-tuple-element.117), channel_id=1, source_target_pairs={{128,64},{129,65},{130,66},{131,67},{132,68},{133,69},{134,70},{13... | collective-permute-start | bytes 786440 | tf_op jit(solution)/shard_map/ppermute | solution.py:352
  111.5 39.8 %collective-permute-start.4 = (bf16[32,4096]{1,0:T(8,128)(2,1)S(1)}, bf16[32,4096]{1,0:T(8,128)(2,1)S(1)}, u32[]{:S(2)}, u32[]{:S(2)}) collective-permute-start(bf16[32,4096]{1,0:T(8,128)(2,1)S(1)} %get-tuple-element.116), channel_id=1, source_target_pairs={{64,0},{128,64},{65,1},{129,65},{66,2},{130,66},{67,3},{131,67},{6... | collective-permute-start | bytes 786440 | tf_op jit(solution)/shard_map/ppermute | solution.py:352
  112.8 46.0 %collective-permute-start.9 = (bf16[32,4096]{1,0:T(8,128)(2,1)S(1)}, bf16[32,4096]{1,0:T(8,128)(2,1)S(1)}, u32[]{:S(2)}, u32[]{:S(2)}) collective-permute-start(bf16[32,4096]{1,0:T(8,128)(2,1)S(1)} %get-tuple-element.130), channel_id=1, source_target_pairs={{64,0},{65,1},{66,2},{67,3},{68,4},{69,5},{70,6},{71,7},{72,8},{73... | collective-permute-start | bytes 786440 | tf_op jit(solution)/shard_map/ppermute | solution.py:352
  114.2 52.1 %collective-permute-start.8 = (bf16[32,4096]{1,0:T(8,128)(2,1)S(1)}, bf16[32,4096]{1,0:T(8,128)(2,1)S(1)}, u32[]{:S(2)}, u32[]{:S(2)}) collective-permute-start(bf16[32,4096]{1,0:T(8,128)(2,1)S(1)} %get-tuple-element.129), channel_id=1, source_target_pairs={{64,0},{65,1},{66,2},{67,3},{68,4},{69,5},{70,6},{71,7},{72,8},{73... | collective-permute-start | bytes 786440 | tf_op jit(solution)/shard_map/ppermute | solution.py:352
  157.5 16.4 %collective-permute-start.7 = (bf16[32,4096]{1,0:T(8,128)(2,1)S(1)}, bf16[32,4096]{1,0:T(8,128)(2,1)S(1)}, u32[]{:S(2)}, u32[]{:S(2)}) collective-permute-start(bf16[32,4096]{1,0:T(8,128)(2,1)S(1)} %get-tuple-element.128), channel_id=1, source_target_pairs={{64,0},{65,1},{66,2},{67,3},{68,4},{69,5},{70,6},{71,7},{72,8},{73... | collective-permute-start | bytes 786440 | tf_op jit(solution)/shard_map/ppermute | solution.py:352
  182.3 6.6 %collective-permute-start.10 = (bf16[256,4096]{1,0:T(8,128)(2,1)}, bf16[256,4096]{1,0:T(8,128)(2,1)}, u32[]{:S(2)}, u32[]{:S(2)}) collective-permute-start(bf16[256,4096]{1,0:T(8,128)(2,1)} %pad_maximum_fusion), channel_id=1, source_target_pairs={{0,1},{1,0},{2,3},{3,2},{4,5},{5,4},{6,7},{7,6},{8,9},{9,8},{10,11... | collective-permute-start | bytes 6291464 | tf_op jit(solution)/shard_map/ppermute | solution.py:31
  194.6 4.8 %collective-permute-start.12 = (bf16[256,256]{1,0:T(8,128)(2,1)S(1)}, bf16[256,256]{1,0:T(8,128)(2,1)S(1)}, u32[]{:S(2)}, u32[]{:S(2)}) collective-permute-start(bf16[256,256]{1,0:T(8,128)(2,1)S(1)} %bitcast.116), channel_id=1, source_target_pairs={{0,14},{2,0},{4,2},{6,4},{8,6},{10,8},{12,10},{14,12},{1,15},{3,1}... | collective-permute-start | bytes 393224 | tf_op jit(solution)/shard_map/ppermute | solution.py:31
  196.3 5.6 %collective-permute-start.11 = (bf16[256,256]{1,0:T(8,128)(2,1)S(1)}, bf16[256,256]{1,0:T(8,128)(2,1)S(1)}, u32[]{:S(2)}, u32[]{:S(2)}) collective-permute-start(bf16[256,256]{1,0:T(8,128)(2,1)S(1)} %bitcast.115), channel_id=1, source_target_pairs={{0,2},{2,4},{4,6},{6,8},{8,10},{10,12},{12,14},{14,0},{1,3},{3,5},... | collective-permute-start | bytes 393224 | tf_op jit(solution)/shard_map/ppermute | solution.py:31
  202.6 6.5 %collective-permute-start.14 = (bf16[512,256]{1,0:T(8,128)(2,1)S(1)}, bf16[512,256]{1,0:T(8,128)(2,1)}, u32[]{:S(2)}, u32[]{:S(2)}) collective-permute-start(bf16[512,256]{1,0:T(8,128)(2,1)S(1)} %fusion.2), channel_id=1, source_target_pairs={{0,14},{2,0},{4,2},{6,4},{8,6},{10,8},{12,10},{14,12},{1,15},{3,1}... | collective-permute-start | bytes 786440 | tf_op jit(solution)/shard_map/ppermute | solution.py:31
  203.0 7.9 %collective-permute-start.13 = (bf16[512,256]{1,0:T(8,128)(2,1)}, bf16[512,256]{1,0:T(8,128)(2,1)}, u32[]{:S(2)}, u32[]{:S(2)}) collective-permute-start(bf16[512,256]{1,0:T(8,128)(2,1)} %fusion.3), channel_id=1, source_target_pairs={{0,2},{2,4},{4,6},{6,8},{8,10},{10,12},{12,14},{14,0},{1,3},{3,5},... | collective-permute-start | bytes 786440 | tf_op jit(solution)/shard_map/ppermute | solution.py:31
  204.1 27.9 %all-to-all-start.4 = ((bf16[4,1024,256]{2,1,0:T(8,128)(2,1)}), bf16[4,1024,256]{2,1,0:T(8,128)(2,1)S(1)}, u32[]{:S(2)}, u32[]{:S(2)}) async-start(bf16[4,1024,256]{2,1,0:T(8,128)(2,1)} %bitcast.107), calls=%async_computation.4 | async-start | bytes 4194304 | tf_op jit(solution)/shard_map/all_to_all | solution.py:62
  212.0 5.6 %collective-permute-start.16 = (bf16[512,256]{1,0:T(8,128)(2,1)S(1)}, bf16[512,256]{1,0:T(8,128)(2,1)S(1)}, u32[]{:S(2)}, u32[]{:S(2)}) collective-permute-start(bf16[512,256]{1,0:T(8,128)(2,1)S(1)} %fusion.1), channel_id=1, source_target_pairs={{0,14},{2,0},{4,2},{6,4},{8,6},{10,8},{12,10},{14,12},{1,15},{3,1}... | collective-permute-start | bytes 786440 | tf_op jit(solution)/shard_map/ppermute | solution.py:31
  213.3 6.7 %collective-permute-start.15 = (bf16[512,256]{1,0:T(8,128)(2,1)S(1)}, bf16[512,256]{1,0:T(8,128)(2,1)S(1)}, u32[]{:S(2)}, u32[]{:S(2)}) collective-permute-start(bf16[512,256]{1,0:T(8,128)(2,1)S(1)} %fusion.4), channel_id=1, source_target_pairs={{0,2},{2,4},{4,6},{6,8},{8,10},{10,12},{12,14},{14,0},{1,3},{3,5},... | collective-permute-start | bytes 786440 | tf_op jit(solution)/shard_map/ppermute | solution.py:31
  220.1 6.8 %collective-permute-start.17 = (bf16[512,256]{1,0:T(8,128)(2,1)S(1)}, bf16[512,256]{1,0:T(8,128)(2,1)S(1)}, u32[]{:S(2)}, u32[]{:S(2)}) collective-permute-start(bf16[512,256]{1,0:T(8,128)(2,1)S(1)} %fusion.5), channel_id=1, source_target_pairs={{0,2},{2,4},{4,6},{6,8},{8,10},{10,12},{12,14},{14,0},{1,3},{3,5},... | collective-permute-start | bytes 786440 | tf_op jit(solution)/shard_map/ppermute | solution.py:31
  220.2 6.7 %collective-permute-start.18 = (bf16[512,256]{1,0:T(8,128)(2,1)S(1)}, bf16[512,256]{1,0:T(8,128)(2,1)S(1)}, u32[]{:S(2)}, u32[]{:S(2)}) collective-permute-start(bf16[512,256]{1,0:T(8,128)(2,1)S(1)} %fusion), channel_id=1, source_target_pairs={{0,14},{2,0},{4,2},{6,4},{8,6},{10,8},{12,10},{14,12},{1,15},{3,1}... | collective-permute-start | bytes 786440 | tf_op jit(solution)/shard_map/ppermute | solution.py:31
  232.0 8.9 %all-to-all-start.6 = ((bf16[4,128,256]{2,1,0:T(8,128)(2,1)}), bf16[4,128,256]{2,1,0:T(8,128)(2,1)S(1)}, u32[]{:S(2)}, u32[]{:S(2)}) async-start(bf16[4,128,256]{2,1,0:T(8,128)(2,1)} %bitcast.29), calls=%async_computation.6 | async-start | bytes 524288 | tf_op jit(solution)/shard_map/all_to_all | solution.py:62
  240.9 16.4 %all-to-all-start.5 = ((bf16[8,128,256]{2,1,0:T(8,128)(2,1)}), bf16[8,128,256]{2,1,0:T(8,128)(2,1)S(1)}, u32[]{:S(2)}, u32[]{:S(2)}) async-start(bf16[8,128,256]{2,1,0:T(8,128)(2,1)} %bitcast.17), calls=%async_computation.5 | async-start | bytes 1048576 | tf_op jit(solution)/shard_map/all_to_all | solution.py:62
  (4 other events, 8.8 us)
Sparse Core Ops, SparseCore 0:
  10.7 87.2 all-gather.2
where the time goes:
time: 277 us; the launch traced here: 276 us
  waiting for transfers between devices  131 us (47%)
  starting transfers between devices  34.5 us (12%)
  blocking collectives  34.2 us (12%)
  Pallas kernels  29.7 us (11%)
  between operations  15.9 us (6%)
  other arithmetic  14.4 us (5%)
  local copies, waits for them, and re-layouts  12 us (4%)
  matrix products  3.95 us (1%)
    all_gather x1, waiting for transfers between devices, local(): full_weight = lax.all_gather(shard, DP, axis=0, tiled=True)  55.2 us
    ppermute x10, waiting for transfers between devices, local(): sent[slot] = lax.ppermute(out, 'section', pairs)  37.1 us
    pallas_call x13, Pallas kernels, tick(): pl.pallas_call(tick_kernel, in_specs=[scalar] * 2 + [spec] * 8 + [pl.Bloc...  27.4 us
    all_to_all x3, waiting for transfers between devices, swapped(): got = lax.all_to_all(blocks.astype(jnp.bfloat16), axis, 0, 0, tiled=True)  20.5 us
    all_to_all x2, blocking collectives, summed(): value = jnp.sum(lax.all_to_all(copies, axis, 0, 0, tiled=True), axis=0)  19.8 us
    ppermute x9, waiting for transfers between devices, shifted(): lax.ppermute(value, axis, [(i, (i + by) % size) for i in range(size)])  15.7 us
    all_to_all x3, starting transfers between devices, swapped(): got = lax.all_to_all(blocks.astype(jnp.bfloat16), axis, 0, 0, tiled=True)  11.7 us
    all_to_all x1, blocking collectives, local(): lax.all_to_all(part.reshape(CORE, -1, width // CORE), 'core', 0, 0, tiled...  10.2 us
  transfers between devices with their start and end apart: 24, of which 15 were waited for; matrix products, arithmetic and copies ran while one was open for 5% of the time, Pallas kernels for 7%

commit v1 on v0

--- a/solution.py
+++ b/solution.py
@@ -68,23 +68,24 @@
 
 def scattered(left, right):
     depth, cols = left.shape[1], right.shape[1]
-    half = cols // 2
+    cut = cols // 4
     unit = depth // (Y * Z)
-    first = jnp.einsum("td,tk->dk", left, right[:, :half], preferred_element_type=jnp.float32)
+    first = jnp.einsum("td,tk->dk", left, right[:, :cut], preferred_element_type=jnp.float32)
     first = first.astype(jnp.bfloat16)
-    later, first = lax.optimization_barrier((right[:, half:], first))
-    first = swapped(first.reshape(Y, Z * unit, half), "y")
+    later, first = lax.optimization_barrier((right[:, cut:], first))
+    first = swapped(first.reshape(Y, Z * unit, cut), "y")
     second = jnp.einsum("td,tk->dk", left, later, preferred_element_type=jnp.float32)
-    second = second.reshape(Y, Z, unit, half)
+    second = second.reshape(Y, Z, unit, cols - cut)
     here = lax.axis_index("z")
 
     def block(offset):
         piece = lax.dynamic_slice_in_dim(second, (here + offset) % Z, 1, 1)
-        return piece.reshape(Y * unit, half)
+        return piece.reshape(Y * unit, cols - cut)
 
     second = ring_scatter(block, Z, "z")
-    first = swapped(first.reshape(Z, unit, half), "z")
-    second = swapped(second.reshape(Y, unit, half), "y")
+    first = swapped(first.reshape(Z, unit, cut), "z")
+    first, second = lax.optimization_barrier((first, second))
+    second = swapped(second.reshape(Y, unit, cols - cut), "y")
     return jnp.concatenate([first, second], axis=1)
 
 

time: 277 us -> 272 us (0.982)
  waiting for transfers between devices: 131 us -> 117 us
  blocking collectives: 34.2 us -> 40.2 us
  other arithmetic: 14.4 us -> 18.2 us
    all_to_all x3 -> x2, waiting for transfers between devices: 20.5 us -> 4.76 us  [swapped(): got = lax.all_to_all(blocks.astype(jnp.bfloat16), axis, 0, 0, tiled=True)]
    all_to_all x0 -> x1, blocking collectives: none -> 9.11 us  [swapped(): got = lax.all_to_all(blocks.astype(jnp.bfloat16), axis, 0, 0, tiled=True)]
    all_to_all x3 -> x2, starting transfers between devices: 11.7 us -> 8.35 us  [swapped(): got = lax.all_to_all(blocks.astype(jnp.bfloat16), axis, 0, 0, tiled=True)]
    all_to_all x1, blocking collectives: 10.2 us -> 7.17 us  [local(): lax.all_to_all(part.reshape(CORE, -1, width // CORE), 'core', 0, 0, tiled...]
    unnamed x10 -> x12, local copies, waits for them, and re-layouts: 5.46 us -> 6.21 us
  transfers between devices with their start and end apart: 24 -> 23, of which waited for: 15 -> 13; matrix products, arithmetic and copies ran while one was open for 5% -> 6% of each run, Pallas kernels for 7% -> 8%
where the time goes in v1:
time: 272 us; the launch traced here: 271 us
  waiting for transfers between devices  117 us (43%)
  blocking collectives  40.2 us (15%)
  starting transfers between devices  32 us (12%)
  Pallas kernels  29.7 us (11%)
  other arithmetic  18.2 us (7%)
  between operations  15.9 us (6%)
  local copies, waits for them, and re-layouts  13.2 us (5%)
  matrix products  4.73 us (2%)
    all_gather x1, waiting for transfers between devices, local(): full_weight = lax.all_gather(shard, DP, axis=0, tiled=True)  55.2 us
    ppermute x10, waiting for transfers between devices, local(): sent[slot] = lax.ppermute(out, 'section', pairs)  37.1 us
    pallas_call x13, Pallas kernels, tick(): pl.pallas_call(tick_kernel, in_specs=[scalar] * 2 + [spec] * 8 + [pl.Bloc...  27.4 us
    all_to_all x2, blocking collectives, summed(): value = jnp.sum(lax.all_to_all(copies, axis, 0, 0, tiled=True), axis=0)  19.8 us
    ppermute x9, waiting for transfers between devices, shifted(): lax.ppermute(value, axis, [(i, (i + by) % size) for i in range(size)])  17.2 us
    ppermute x9, starting transfers between devices, shifted(): lax.ppermute(value, axis, [(i, (i + by) % size) for i in range(size)])  10.2 us
    ppermute x10, starting transfers between devices, local(): sent[slot] = lax.ppermute(out, 'section', pairs)  9.23 us
    all_to_all x1, blocking collectives, swapped(): got = lax.all_to_all(blocks.astype(jnp.bfloat16), axis, 0, 0, tiled=True)  9.11 us
  transfers between devices with their start and end apart: 23, of which 13 were waited for; matrix products, arithmetic and copies ran while one was open for 6% of the time, Pallas kernels for 8%

profile of v1, /device:TPU:1, one launch (start us, length us, event | category | flops | bytes accessed | tf_op | source)
XLA Modules:
  0.0 270.7 jit_solution(1261427502937304358)
XLA Ops:
  10.6 6.6 %all_to_all.40 = f32[2,8,128]{2,1,0:T(8,128)S(1)} all-to-all(f32[2,8,128]{2,1,0:T(8,128)S(1)} %broadcast_in_dim.68), channel_id=1, replica_groups=mesh['section'=4,'y'=4,'z'=8,'core'=2] {'core'}, dimensions={0} | all-to-all | bytes 16384 | tf_op jit(solution)/shard_map/all_to_all | solution.py:38
  17.1 13.2 %all_to_all.41 = f32[8,8,128]{2,1,0:T(8,128)S(1)} all-to-all(f32[8,8,128]{2,1,0:T(8,128)S(1)} %broadcast_in_dim.69), channel_id=1, replica_groups=mesh['section'=4,'y'=4,'z'=8,'core'=2] {'z'}, dimensions={0} | all-to-all | bytes 65536 | tf_op jit(solution)/shard_map/all_to_all | solution.py:38
  31.0 4.2 %all-to-all-start.2 = ((f32[4,8,128]{2,1,0:T(8,128)}), f32[4,8,128]{2,1,0:T(8,128)S(1)}, u32[]{:S(2)}, u32[]{:S(2)}) async-start(f32[4,8,128]{2,1,0:T(8,128)} %broadcast_in_dim.70), calls=%async_computation.2 | async-start | bytes 32768 | tf_op jit(solution)/shard_map/all_to_all | solution.py:38
  42.8 55.2 %all-gather.3.cloned.1.call-done = bf16[1,4096,1024]{2,1,0:T(8,128)(2,1)} async-done(((bf16[1,64,1024]{2,1,0:T(8,128)(2,1)}), bf16[1,4096,1024]{2,1,0:T(8,128)(2,1)}) %all-gather.3.cloned.1.call-update) | async-done | bytes 8388624 | tf_op jit(solution)/shard_map/all_gather | solution.py:323
  98.0 3.4 %copy-done = bf16[1,4096,1024]{2,1,0:T(8,128)(2,1)S(1)} copy-done((bf16[1,4096,1024]{2,1,0:T(8,128)(2,1)S(1)}, bf16[1,4096,1024]{2,1,0:T(8,128)(2,1)}, u32[]{:S(2)}) %copy-start) | copy-done | bytes 8388632
  103.3 2.2 forward.1
  115.5 35.8 %collective-permute-done.4.came_ref = bf16[32,4096]{1,0:T(8,128)(2,1)S(1)} collective-permute-done((bf16[32,4096]{1,0:T(8,128)(2,1)S(1)}, bf16[32,4096]{1,0:T(8,128)(2,1)S(1)}, u32[]{:S(2)}, u32[]{:S(2)}) %collective-permute-start.4) | collective-permute-done | bytes 262176 | tf_op jit(solution)/shard_map/ppermute | solution.py:353
  151.3 6.2 %tick.22 = (bf16[32,4096]{1,0:T(8,128)(2,1)S(1)}, bf16[128,4096]{1,0:T(8,128)(2,1)}, bf16[128,4096]{1,0:T(8,128)(2,1)S(1)}, bf16[128,1024]{1,0:T(8,128)(2,1)S(1)}) custom-call(s32[1]{0:T(128)S(6)} %add.272.index_ref, s32[1]{0:T(128)} %bitcast.section_ref, ...), custom_call_target="tpu_custom_call", output_to_operand_aliasing={{1}: (10, {}), {2}: (11, {}), {3}: (12, {})} | custom-call | flops 2147483648 | bytes 8388608 | tf_op jit(solution)/shard_map/tick/pallas_call | solution.py:268
  158.8 6.9 %tick.23 = (bf16[32,4096]{1,0:T(8,128)(2,1)}, bf16[128,4096]{1,0:T(8,128)(2,1)}, bf16[128,4096]{1,0:T(8,128)(2,1)S(1)}, bf16[128,1024]{1,0:T(8,128)(2,1)S(1)}) custom-call(s32[1]{0:T(128)S(6)} %add.300.index_ref, s32[1]{0:T(128)} %bitcast.section_ref, ...), custom_call_target="tpu_custom_call", output_to_operand_aliasing={{1}: (10, {}), {2}: (11, {}), {3}: (12, {})} | custom-call | flops 2147483648 | bytes 8388608 | tf_op jit(solution)/shard_map/tick/pallas_call | solution.py:268
  166.3 6.9 %tick.24 = (bf16[32,4096]{1,0:T(8,128)(2,1)}, bf16[128,4096]{1,0:T(8,128)(2,1)}, bf16[128,4096]{1,0:T(8,128)(2,1)S(1)}, bf16[128,1024]{1,0:T(8,128)(2,1)S(1)}) custom-call(s32[1]{0:T(128)S(6)} %add.298.index_ref, s32[1]{0:T(128)} %bitcast.section_ref, ...), custom_call_target="tpu_custom_call", output_to_operand_aliasing={{1}: (10, {}), {2}: (11, {}), {3}: (12, {})} | custom-call | flops 2147483648 | bytes 8388608 | tf_op jit(solution)/shard_map/tick/pallas_call | solution.py:268
  173.9 6.9 %tick.25 = (bf16[32,4096]{1,0:T(8,128)(2,1)}, bf16[128,4096]{1,0:T(8,128)(2,1)}, bf16[128,4096]{1,0:T(8,128)(2,1)S(1)}, bf16[128,1024]{1,0:T(8,128)(2,1)S(1)}) custom-call(s32[1]{0:T(128)S(6)} %add.271.index_ref, s32[1]{0:T(128)} %bitcast.section_ref, ...), custom_call_target="tpu_custom_call", output_to_operand_aliasing={{1}: (10, {}), {2}: (11, {}), {3}: (12, {})} | custom-call | flops 2147483648 | bytes 8388608 | tf_op jit(solution)/shard_map/tick/pallas_call | solution.py:268
  184.4 4.2 %all_to_all.42 = bf16[2,256,512]{2,1,0:T(8,128)(2,1)S(1)} all-to-all(bf16[2,256,512]{2,1,0:T(8,128)(2,1)S(1)} %bitcast.110), channel_id=1, replica_groups=mesh['section'=4,'y'=4,'z'=8,'core'=2] {'core'}, dimensions={0} | all-to-all | bytes 1048576 | tf_op jit(solution)/shard_map/all_to_all | solution.py:358
  190.6 2.3 convolution_convert_fusion
  192.9 2.4 fusion.10
  198.8 2.8 %collective-permute-done.12 = bf16[256,384]{1,0:T(8,128)(2,1)S(1)} collective-permute-done((bf16[256,384]{1,0:T(8,128)(2,1)S(1)}, bf16[256,384]{1,0:T(8,128)(2,1)S(1)}, u32[]{:S(2)}, u32[]{:S(2)}) %collective-permute-start.12) | collective-permute-done | bytes 196640 | tf_op jit(solution)/shard_map/ppermute | solution.py:31
  206.4 3.5 %all-to-all-start.4 = ((bf16[4,1024,128]{2,1,0:T(8,128)(2,1)}), bf16[4,1024,128]{2,1,0:T(8,128)(2,1)S(1)}, u32[]{:S(2)}, u32[]{:S(2)}) async-start(bf16[4,1024,128]{2,1,0:T(8,128)(2,1)} %bitcast.16), calls=%async_computation.4 | async-start | bytes 2097152 | tf_op jit(solution)/shard_map/all_to_all | solution.py:62
  209.9 4.5 %collective-permute-done.14 = bf16[512,384]{1,0:T(8,128)(2,1)} collective-permute-done((bf16[512,384]{1,0:T(8,128)(2,1)}, bf16[512,384]{1,0:T(8,128)(2,1)}, u32[]{:S(2)}, u32[]{:S(2)}) %collective-permute-start.14) | collective-permute-done | bytes 393248 | tf_op jit(solution)/shard_map/ppermute | solution.py:31
  214.4 2.1 fusion.1
  218.6 2.3 collective-permute-start.16
  223.8 4.8 %all-to-all-start.5 = ((bf16[8,128,128]{2,1,0:T(8,128)(2,1)}), bf16[8,128,128]{2,1,0:T(8,128)(2,1)S(1)}, u32[]{:S(2)}, u32[]{:S(2)}) async-start(bf16[8,128,128]{2,1,0:T(8,128)(2,1)} %bitcast.17), calls=%async_computation.5 | async-start | bytes 524288 | tf_op jit(solution)/shard_map/all_to_all | solution.py:62
  234.7 2.7 all-to-all-done.5
  237.4 7.7 %collective-permute-done.17 = bf16[512,384]{1,0:T(8,128)(2,1)S(1)} collective-permute-done((bf16[512,384]{1,0:T(8,128)(2,1)S(1)}, bf16[512,384]{1,0:T(8,128)(2,1)S(1)}, u32[]{:S(2)}, u32[]{:S(2)}) %collective-permute-start.17) | collective-permute-done | bytes 393248 | tf_op jit(solution)/shard_map/ppermute | solution.py:31
  246.4 9.1 %all_to_all.43 = bf16[4,128,384]{2,1,0:T(8,128)(2,1)S(1)} all-to-all(bf16[4,128,384]{2,1,0:T(8,128)(2,1)S(1)} %bitcast.111), channel_id=1, replica_groups=mesh['section'=4,'y'=4,'z'=8,'core'=2] {'y'}, dimensions={0} | all-to-all | bytes 786432 | tf_op jit(solution)/shard_map/all_to_all | solution.py:62
  255.6 7.2 %all_to_all.44 = f32[2,64,512]{2,1,0:T(8,128)S(1)} all-to-all(f32[2,64,512]{2,1,0:T(8,128)S(1)} %maximum_multiply_fusion), channel_id=1, replica_groups=mesh['section'=4,'y'=4,'z'=8,'core'=2] {'core'}, dimensions={0} | all-to-all | bytes 524288 | tf_op jit(solution)/shard_map/all_to_all | solution.py:362
  (103 shorter events, 51.8 us)
Async XLA Ops:
  7.2 90.8 %all-gather.3.cloned.1.call-start = ((), (), s32[]{:S(2)}) async-start(), calls=%async_computation.8 | async-start | bytes 8519680 | tf_op jit(solution)/shard_map/all_gather | solution.py:323
  31.0 8.4 %all-to-all-start.2 = ((f32[4,8,128]{2,1,0:T(8,128)}), f32[4,8,128]{2,1,0:T(8,128)S(1)}, u32[]{:S(2)}, u32[]{:S(2)}) async-start(f32[4,8,128]{2,1,0:T(8,128)} %broadcast_in_dim.70), calls=%async_computation.2 | async-start | bytes 32768 | tf_op jit(solution)/shard_map/all_to_all | solution.py:38
  103.3 3.4 %copy-start.2 = (bf16[128,4096]{1,0:T(8,128)(2,1)S(1)}, bf16[128,4096]{1,0:T(8,128)(2,1)}, u32[]{:S(2)}) copy-start(bf16[128,4096]{1,0:T(8,128)(2,1)} %top_ref.25) | copy-start | bytes 3145732
  106.8 2.2 collective-permute-start
  107.6 2.2 collective-permute-start.3
  108.3 2.2 collective-permute-start.2
  109.1 2.2 collective-permute-start.1
  109.8 3.0 %collective-permute-start.6 = (bf16[32,4096]{1,0:T(8,128)(2,1)S(1)}, bf16[32,4096]{1,0:T(8,128)(2,1)S(1)}, u32[]{:S(2)}, u32[]{:S(2)}) collective-permute-start(bf16[32,4096]{1,0:T(8,128)(2,1)S(1)} %get-tuple-element.120), channel_id=1, source_target_pairs={{128,64},{129,65},{130,66},{131,67},{132,68},{133,69},{134,70},{13... | collective-permute-start | bytes 786440 | tf_op jit(solution)/shard_map/ppermute | solution.py:353
  110.5 3.6 %collective-permute-start.5 = (bf16[32,4096]{1,0:T(8,128)(2,1)S(1)}, bf16[32,4096]{1,0:T(8,128)(2,1)S(1)}, u32[]{:S(2)}, u32[]{:S(2)}) collective-permute-start(bf16[32,4096]{1,0:T(8,128)(2,1)S(1)} %get-tuple-element.119), channel_id=1, source_target_pairs={{128,64},{129,65},{130,66},{131,67},{132,68},{133,69},{134,70},{13... | collective-permute-start | bytes 786440 | tf_op jit(solution)/shard_map/ppermute | solution.py:353
  111.5 39.8 %collective-permute-start.4 = (bf16[32,4096]{1,0:T(8,128)(2,1)S(1)}, bf16[32,4096]{1,0:T(8,128)(2,1)S(1)}, u32[]{:S(2)}, u32[]{:S(2)}) collective-permute-start(bf16[32,4096]{1,0:T(8,128)(2,1)S(1)} %get-tuple-element.118), channel_id=1, source_target_pairs={{64,0},{128,64},{65,1},{129,65},{66,2},{130,66},{67,3},{131,67},{6... | collective-permute-start | bytes 786440 | tf_op jit(solution)/shard_map/ppermute | solution.py:353
  112.8 46.0 %collective-permute-start.9 = (bf16[32,4096]{1,0:T(8,128)(2,1)S(1)}, bf16[32,4096]{1,0:T(8,128)(2,1)S(1)}, u32[]{:S(2)}, u32[]{:S(2)}) collective-permute-start(bf16[32,4096]{1,0:T(8,128)(2,1)S(1)} %get-tuple-element.132), channel_id=1, source_target_pairs={{64,0},{65,1},{66,2},{67,3},{68,4},{69,5},{70,6},{71,7},{72,8},{73... | collective-permute-start | bytes 786440 | tf_op jit(solution)/shard_map/ppermute | solution.py:353
  114.2 52.1 %collective-permute-start.8 = (bf16[32,4096]{1,0:T(8,128)(2,1)S(1)}, bf16[32,4096]{1,0:T(8,128)(2,1)S(1)}, u32[]{:S(2)}, u32[]{:S(2)}) collective-permute-start(bf16[32,4096]{1,0:T(8,128)(2,1)S(1)} %get-tuple-element.131), channel_id=1, source_target_pairs={{64,0},{65,1},{66,2},{67,3},{68,4},{69,5},{70,6},{71,7},{72,8},{73... | collective-permute-start | bytes 786440 | tf_op jit(solution)/shard_map/ppermute | solution.py:353
  157.5 16.4 %collective-permute-start.7 = (bf16[32,4096]{1,0:T(8,128)(2,1)S(1)}, bf16[32,4096]{1,0:T(8,128)(2,1)S(1)}, u32[]{:S(2)}, u32[]{:S(2)}) collective-permute-start(bf16[32,4096]{1,0:T(8,128)(2,1)S(1)} %get-tuple-element.130), channel_id=1, source_target_pairs={{64,0},{65,1},{66,2},{67,3},{68,4},{69,5},{70,6},{71,7},{72,8},{73... | collective-permute-start | bytes 786440 | tf_op jit(solution)/shard_map/ppermute | solution.py:353
  182.3 6.6 %collective-permute-start.10 = (bf16[256,4096]{1,0:T(8,128)(2,1)}, bf16[256,4096]{1,0:T(8,128)(2,1)}, u32[]{:S(2)}, u32[]{:S(2)}) collective-permute-start(bf16[256,4096]{1,0:T(8,128)(2,1)} %pad_maximum_fusion), channel_id=1, source_target_pairs={{0,1},{1,0},{2,3},{3,2},{4,5},{5,4},{6,7},{7,6},{8,9},{9,8},{10,11... | collective-permute-start | bytes 6291464 | tf_op jit(solution)/shard_map/ppermute | solution.py:31
  195.5 6.2 %collective-permute-start.12 = (bf16[256,384]{1,0:T(8,128)(2,1)S(1)}, bf16[256,384]{1,0:T(8,128)(2,1)S(1)}, u32[]{:S(2)}, u32[]{:S(2)}) collective-permute-start(bf16[256,384]{1,0:T(8,128)(2,1)S(1)} %bitcast.116), channel_id=1, source_target_pairs={{0,14},{2,0},{4,2},{6,4},{8,6},{10,8},{12,10},{14,12},{1,15},{3,1}... | collective-permute-start | bytes 589832 | tf_op jit(solution)/shard_map/ppermute | solution.py:31
  197.1 7.0 %collective-permute-start.11 = (bf16[256,384]{1,0:T(8,128)(2,1)S(1)}, bf16[256,384]{1,0:T(8,128)(2,1)S(1)}, u32[]{:S(2)}, u32[]{:S(2)}) collective-permute-start(bf16[256,384]{1,0:T(8,128)(2,1)S(1)} %bitcast.115), channel_id=1, source_target_pairs={{0,2},{2,4},{4,6},{6,8},{8,10},{10,12},{12,14},{14,0},{1,3},{3,5},... | collective-permute-start | bytes 589832 | tf_op jit(solution)/shard_map/ppermute | solution.py:31
  204.9 9.5 %collective-permute-start.14 = (bf16[512,384]{1,0:T(8,128)(2,1)}, bf16[512,384]{1,0:T(8,128)(2,1)}, u32[]{:S(2)}, u32[]{:S(2)}) collective-permute-start(bf16[512,384]{1,0:T(8,128)(2,1)} %fusion.2), channel_id=1, source_target_pairs={{0,14},{2,0},{4,2},{6,4},{8,6},{10,8},{12,10},{14,12},{1,15},{3,1}... | collective-permute-start | bytes 1179656 | tf_op jit(solution)/shard_map/ppermute | solution.py:31
  206.0 10.7 %collective-permute-start.13 = (bf16[512,384]{1,0:T(8,128)(2,1)}, bf16[512,384]{1,0:T(8,128)(2,1)}, u32[]{:S(2)}, u32[]{:S(2)}) collective-permute-start(bf16[512,384]{1,0:T(8,128)(2,1)} %fusion.3), channel_id=1, source_target_pairs={{0,2},{2,4},{4,6},{6,8},{8,10},{10,12},{12,14},{14,0},{1,3},{3,5},... | collective-permute-start | bytes 1179656 | tf_op jit(solution)/shard_map/ppermute | solution.py:31
  206.4 16.6 %all-to-all-start.4 = ((bf16[4,1024,128]{2,1,0:T(8,128)(2,1)}), bf16[4,1024,128]{2,1,0:T(8,128)(2,1)S(1)}, u32[]{:S(2)}, u32[]{:S(2)}) async-start(bf16[4,1024,128]{2,1,0:T(8,128)(2,1)} %bitcast.16), calls=%async_computation.4 | async-start | bytes 2097152 | tf_op jit(solution)/shard_map/all_to_all | solution.py:62
  218.6 10.1 %collective-permute-start.16 = (bf16[512,384]{1,0:T(8,128)(2,1)}, bf16[512,384]{1,0:T(8,128)(2,1)S(1)}, u32[]{:S(2)}, u32[]{:S(2)}) collective-permute-start(bf16[512,384]{1,0:T(8,128)(2,1)} %fusion.1), channel_id=1, source_target_pairs={{0,14},{2,0},{4,2},{6,4},{8,6},{10,8},{12,10},{14,12},{1,15},{3,1}... | collective-permute-start | bytes 1179656 | tf_op jit(solution)/shard_map/ppermute | solution.py:31
  220.9 9.8 %collective-permute-start.15 = (bf16[512,384]{1,0:T(8,128)(2,1)}, bf16[512,384]{1,0:T(8,128)(2,1)}, u32[]{:S(2)}, u32[]{:S(2)}) collective-permute-start(bf16[512,384]{1,0:T(8,128)(2,1)} %fusion.4), channel_id=1, source_target_pairs={{0,2},{2,4},{4,6},{6,8},{8,10},{10,12},{12,14},{14,0},{1,3},{3,5},... | collective-permute-start | bytes 1179656 | tf_op jit(solution)/shard_map/ppermute | solution.py:31
  223.8 13.5 %all-to-all-start.5 = ((bf16[8,128,128]{2,1,0:T(8,128)(2,1)}), bf16[8,128,128]{2,1,0:T(8,128)(2,1)S(1)}, u32[]{:S(2)}, u32[]{:S(2)}) async-start(bf16[8,128,128]{2,1,0:T(8,128)(2,1)} %bitcast.17), calls=%async_computation.5 | async-start | bytes 524288 | tf_op jit(solution)/shard_map/all_to_all | solution.py:62
  231.9 13.2 %collective-permute-start.17 = (bf16[512,384]{1,0:T(8,128)(2,1)S(1)}, bf16[512,384]{1,0:T(8,128)(2,1)S(1)}, u32[]{:S(2)}, u32[]{:S(2)}) collective-permute-start(bf16[512,384]{1,0:T(8,128)(2,1)S(1)} %fusion.5), channel_id=1, source_target_pairs={{0,2},{2,4},{4,6},{6,8},{8,10},{10,12},{12,14},{14,0},{1,3},{3,5},... | collective-permute-start | bytes 1179656 | tf_op jit(solution)/shard_map/ppermute | solution.py:31
  233.2 11.9 %collective-permute-start.18 = (bf16[512,384]{1,0:T(8,128)(2,1)S(1)}, bf16[512,384]{1,0:T(8,128)(2,1)S(1)}, u32[]{:S(2)}, u32[]{:S(2)}) collective-permute-start(bf16[512,384]{1,0:T(8,128)(2,1)S(1)} %fusion), channel_id=1, source_target_pairs={{0,14},{2,0},{4,2},{6,4},{8,6},{10,8},{12,10},{14,12},{1,15},{3,1}... | collective-permute-start | bytes 1179656 | tf_op jit(solution)/shard_map/ppermute | solution.py:31
  (4 other events, 6.1 us)
Sparse Core Ops, SparseCore 0:
  10.7 87.2 all-gather.2
